TPU v7x, 256 devices: a whole 4x4x8 slice. The times are simulated.
256 devices in a mesh: rep: 4 (over y), fsdp: 64 (over x, z, core).
Axes of the slice: x: 4, y: 4, z: 8, core: 2. Of those that a mesh axis runs over, the one named last changes fastest.
Arguments:
- activations: bfloat16 [65536, 512], P(('rep', 'fsdp')), may hold values from -6 to 6
- output_grads: bfloat16 [65536, 8192], P(('rep', 'fsdp'))
- master: float32 [8192, 512], P('fsdp'), may hold values from -6 to 6
- first_moment: float32 [8192, 512], P('fsdp'), may hold values from -4 to 4
- second_moment: float32 [8192, 512], P('fsdp'), may hold values from 0.2 to 2
Outputs:
- new_master: float32 [8192, 512], P('fsdp')
- new_first: float32 [8192, 512], P('fsdp')
- new_second: float32 [8192, 512], P('fsdp')
- params: bfloat16 [8192, 512], replicated
All inputs are finite; a program needn't handle non-finite values.
Results may differ from a plain program's by a relative error of at most 0.0004.
Values may be sent and summed in bfloat16 or wider, within the bound.
No kernel may reach another device: no remote copies, remote signals or barrier semaphores. Data moves between devices by JAX's collectives and lax.ppermute only.
A program may use at most 128 MiB of HBM per device.

v0:
```python
import jax
import jax.numpy as jnp
from jax import lax
from jax.sharding import PartitionSpec as P

dot_epsilon = 1e-06
beta_one = 0.9
beta_two = 0.95
adam_epsilon = 1e-08
learn_rate = 0.02
decay_rate = 0.1
contract_first = (((0,), (0,)), ((), ()))


def swapped(shard, axis, apart):
    return lax.ppermute(shard, axis, [(i, i ^ 1 << apart) for i in range(lax.axis_size(axis))])


def reversed_bits(number_in, bit_count):
    result = 0
    for position in range(bit_count):
        result = result << 1 | number_in >> position & 1
    return result


def local(activations, output_grads, master, first_moment, second_moment):
    grad_shard = lax.psum_scatter(
        lax.dot_general(
            output_grads, activations, contract_first, preferred_element_type=jnp.float32
        ),
        "fsdp",
        scatter_dimension=0,
        tiled=True,
    )
    replica_count = lax.axis_size("rep")
    level_total = replica_count.bit_length() - 1
    replica = lax.axis_index("rep")
    current = grad_shard
    for level_index in range(level_total):
        side_bit = replica >> level_index & 1
        low_side = side_bit == 0
        half_rows = current.shape[0] // 2
        lower_half = current[:half_rows]
        upper_half = current[half_rows:]
        kept_rows = jnp.where(low_side, lower_half, upper_half)
        outgoing = jnp.where(low_side, upper_half, lower_half)
        incoming = swapped(outgoing, "rep", level_index)
        left_vec = jnp.where(low_side, kept_rows, incoming)
        right_vec = jnp.where(low_side, incoming, kept_rows)
        partial_dots = jnp.stack(
            [
                jnp.sum(left_vec * right_vec),
                jnp.sum(left_vec * left_vec),
                jnp.sum(right_vec * right_vec),
            ]
        )
        totals = lax.psum(partial_dots, "fsdp")
        for inner_bit in range(level_index + 1):
            totals = totals + swapped(totals, "rep", inner_bit)
        left_coef = 1.0 - totals[0] / (2.0 * (totals[1] + dot_epsilon))
        right_coef = 1.0 - totals[0] / (2.0 * (totals[2] + dot_epsilon))
        current = left_coef * left_vec + right_coef * right_vec
    piece_rows = current.shape[0]
    gathered = lax.all_gather(current, "rep", axis=0, tiled=True)
    ordered = [
        gathered[
            reversed_bits(place, level_total)
            * piece_rows : (reversed_bits(place, level_total) + 1)
            * piece_rows
        ]
        for place in range(replica_count)
    ]
    combined = jnp.concatenate(ordered, axis=0)
    correct_one = 1.0 - (beta_one**50) ** 2
    correct_two = 1.0 - (beta_two**50) ** 2
    new_first = beta_one * first_moment + (1.0 - beta_one) * combined
    new_second = beta_two * second_moment + (1.0 - beta_two) * combined * combined
    update = (
        new_first / correct_one / (jnp.sqrt(new_second / correct_two) + adam_epsilon)
        + decay_rate * master
    )
    new_master = master - learn_rate * update
    params = lax.all_gather(new_master.astype(jnp.bfloat16), "fsdp", axis=0, tiled=True)
    return (new_master, new_first, new_second, params)


def solution(mesh):
    in_specs = (
        P(("rep", "fsdp"), None),
        P(("rep", "fsdp"), None),
        P("fsdp", None),
        P("fsdp", None),
        P("fsdp", None),
    )
    out_specs = (P("fsdp", None), P("fsdp", None), P("fsdp", None), P())
    return jax.shard_map(local, mesh=mesh, in_specs=in_specs, out_specs=out_specs, check_vma=False)
```

profile of v0, /device:TPU:1, one launch (start us, length us, event | category | flops | bytes accessed | tf_op | source)
XLA Modules:
  0.0 601.0 jit_solution(10944400333961210456)
XLA Ops:
  7.2 0.0 copy-start
  7.2 0.0 reduce-scatter.2.cloned.1.call-start
  7.2 0.9 copy-done
  8.1 10.3 %fusion.6 = f32[8192,512]{1,0:T(8,128)} fusion(bf16[256,8192]{1,0:T(8,128)(2,1)} %param.6, bf16[256,512]{1,0:T(8,128)(2,1)S(1)} %copy-done), kind=kOutput, calls=%fused_computation.27 | convolution fusion | flops 2147483648 | bytes 21233664 | tf_op jit(solution)/shard_map/dot_general | solution.py:28
  18.4 0.0 copy-start.1
  18.4 0.0 copy-start.2
  18.4 0.0 copy-start.3
  18.4 0.0 reduce-scatter.2.cloned.1.call-update
  18.4 0.0 all-gather.2.cloned.1.call-start
  18.5 189.2 %reduce-scatter.2.cloned.1.call-done = f32[128,512]{1,0:T(8,128)} async-done(((f32[8192,512]{1,0:T(8,128)}), f32[128,512]{1,0:T(8,128)}) %reduce-scatter.2.cloned.1.call-update) | async-done | bytes 262160 | tf_op jit(solution)/shard_map/reduce_scatter | solution.py:27
  207.7 1.0 slice_select_fusion
  208.7 0.9 collective-permute-start
  209.6 3.0 collective-permute-done
  212.6 1.6 multiply_reduce_fusion.2
  214.2 2.0 pad_maximum_fusion.1
  216.2 129.1 %psum.14 = f32[3]{0:T(128)S(1)} all-reduce(f32[3]{0:T(128)S(1)} %pad_maximum_fusion.1), channel_id=1, replica_groups=mesh['rep'=4,'fsdp'=64] {'fsdp'}, use_global_device_ids=true, to_apply=%region_4.5 | all-reduce | flops 3 | bytes 24 | tf_op jit(solution)/shard_map/psum | solution.py:57
  345.3 1.3 collective-permute-start.1
  346.6 1.2 collective-permute-done.1
  347.8 0.6 fusion.5
  351.0 2.6 collective-permute-start.2
  353.7 2.1 collective-permute-done.2
  355.7 0.6 multiply_reduce_fusion.5
  356.4 2.0 pad_maximum_fusion.2
  358.4 126.3 %psum.15 = f32[3]{0:T(128)S(1)} all-reduce(f32[3]{0:T(128)S(1)} %pad_maximum_fusion.2), channel_id=1, replica_groups=mesh['rep'=4,'fsdp'=64] {'fsdp'}, use_global_device_ids=true, to_apply=%region_8.9 | all-reduce | flops 3 | bytes 24 | tf_op jit(solution)/shard_map/psum | solution.py:57
  484.7 1.3 collective-permute-start.3
  486.0 1.2 collective-permute-done.3
  487.2 2.5 collective-permute-start.4
  489.7 1.3 collective-permute-done.4
  491.1 0.6 fusion.4
  494.3 9.5 %all_gather.6 = f32[128,512]{1,0:T(8,128)S(1)} all-gather(f32[32,512]{1,0:T(8,128)S(1)} %multiply_add_fusion.2), channel_id=1, replica_groups=mesh['rep'=4,'fsdp'=64] {'rep'}, dimensions={0}, use_global_device_ids=true | all-gather | bytes 327680 | tf_op jit(solution)/shard_map/all_gather | solution.py:64
  503.8 0.0 copy-done.1
  503.8 0.0 copy-done.2
  503.9 0.0 copy-done.3
  503.9 1.1 fusion.1
  504.9 0.0 all-gather.2.cloned.1.call-update
  504.9 81.9 %all-gather.2.cloned.1.call-done = bf16[8192,512]{1,0:T(8,128)(2,1)} async-done(((bf16[128,512]{1,0:T(8,128)(2,1)}), bf16[8192,512]{1,0:T(8,128)(2,1)}) %all-gather.2.cloned.1.call-update) | async-done | bytes 8388624 | tf_op jit(solution)/shard_map/all_gather | solution.py:83
  586.9 7.3 %copy.10 = bf16[8192,512]{1,0:T(8,128)(2,1)} copy(bf16[8192,512]{1,0:T(8,128)(2,1)} %all-gather.2.cloned.1.call-done) | data formatting | bytes 16777216
  (7 shorter events, 0.1 us)
Async XLA Ops:
  7.2 1.0 copy-start
  7.2 200.5 %reduce-scatter.2.cloned.1.call-start = ((), (), s32[]{:S(2)}) async-start(), calls=%async_computation.1 | async-start | bytes 17039360 | tf_op jit(solution)/shard_map/reduce_scatter | solution.py:27
  18.4 485.4 %copy-start.1 = (f32[128,512]{1,0:T(8,128)S(1)}, f32[128,512]{1,0:T(8,128)}, u32[]{:S(2)}) copy-start(f32[128,512]{1,0:T(8,128)} %param.7) | copy-start | bytes 786436
  18.4 485.4 %copy-start.2 = (f32[128,512]{1,0:T(8,128)S(1)}, f32[128,512]{1,0:T(8,128)}, u32[]{:S(2)}) copy-start(f32[128,512]{1,0:T(8,128)} %param.8) | copy-start | bytes 786436
  18.4 485.5 %copy-start.3 = (f32[128,512]{1,0:T(8,128)S(1)}, f32[128,512]{1,0:T(8,128)}, u32[]{:S(2)}) copy-start(f32[128,512]{1,0:T(8,128)} %param.9) | copy-start | bytes 786436
  18.4 568.4 %all-gather.2.cloned.1.call-start = ((), (), s32[]{:S(2)}) async-start(), calls=%async_computation.2 | async-start | bytes 8519680 | tf_op jit(solution)/shard_map/all_gather | solution.py:83
  208.7 3.9 collective-permute-start
  345.3 2.5 collective-permute-start.1
  351.0 4.7 collective-permute-start.2
  484.7 2.5 collective-permute-start.3
  487.2 3.9 collective-permute-start.4
Sparse Core Ops, SparseCore 0:
  18.6 189.1 reduce-scatter.1
  505.1 81.7 all-gather.1
where the time goes:
time: 601 us
  waiting for transfers between devices  280 us (47%)
  blocking collectives  265 us (44%)
  between operations  19.3 us (3%)
  matrix products  10.3 us (2%)
  local copies, waits for them, and re-layouts  9.44 us (2%)
  starting transfers between devices  8.68 us (1%)
  other arithmetic  8.38 us (1%)
    psum x2, blocking collectives, local(): totals = lax.psum(partial_dots, 'fsdp')  255 us
    reduce_scatter x1, waiting for transfers between devices, local(): lax.psum_scatter(lax.dot_general(output_grads, activations, contract_firs...  189 us
    all_gather x1, waiting for transfers between devices, local(): lax.all_gather(new_master.astype(jnp.bfloat16), 'fsdp', axis=0, tiled=True)  81.9 us
  transfers between devices with their start and end apart: 7, of which 7 were waited for; matrix products, arithmetic and copies ran while one was open for 0% of the time, Pallas kernels for 0%

commit v1 on v0

--- a/solution.py
+++ b/solution.py
@@ -10,6 +10,12 @@
 learn_rate = 0.02
 decay_rate = 0.1
 contract_first = (((0,), (0,)), ((), ()))
+
+
+def gather_from_all(x, axis, dim):
+    size = lax.axis_size(axis)
+    repeats = [size if d == dim else 1 for d in range(x.ndim)]
+    return lax.all_to_all(jnp.tile(x, repeats), axis, split_axis=dim, concat_axis=dim, tiled=True)
 
 
 def swapped(shard, axis, apart):
@@ -80,7 +86,7 @@
         + decay_rate * master
     )
     new_master = master - learn_rate * update
-    params = lax.all_gather(new_master.astype(jnp.bfloat16), "fsdp", axis=0, tiled=True)
+    params = gather_from_all(new_master.astype(jnp.bfloat16), "fsdp", 0)
     return (new_master, new_first, new_second, params)
 
 

time: 601 us -> 717 us (1.19)
  blocking collectives: 265 us -> 461 us
  waiting for transfers between devices: 280 us -> 198 us
    all_to_all x0 -> x1, blocking collectives: none -> 196 us  [gather_from_all(): lax.all_to_all(jnp.tile(x, repeats), axis, split_axis=dim, concat_axis=di...]
    all_gather x1 -> x0, waiting for transfers between devices: 81.9 us -> none  [local(): lax.all_gather(new_master.astype(jnp.bfloat16), 'fsdp', axis=0, tiled=True)]
  transfers between devices with their start and end apart: 7 -> 6, of which waited for: 7 -> 6; matrix products, arithmetic and copies ran while one was open for 0% -> 0% of each run, Pallas kernels for 0% -> 0%
where the time goes in v1:
time: 717 us; the launch traced here: 716 us
  blocking collectives  461 us (64%)
  waiting for transfers between devices  198 us (28%)
  between operations  19.3 us (3%)
  local copies, waits for them, and re-layouts  10.4 us (1%)
  matrix products  10.3 us (1%)
  starting transfers between devices  8.64 us (1%)
  other arithmetic  8.34 us (1%)
    psum x2, blocking collectives, local(): totals = lax.psum(partial_dots, 'fsdp')  255 us
    all_to_all x1, blocking collectives, gather_from_all(): lax.all_to_all(jnp.tile(x, repeats), axis, split_axis=dim, concat_axis=di...  196 us
    reduce_scatter x1, waiting for transfers between devices, local(): lax.psum_scatter(lax.dot_general(output_grads, activations, contract_firs...  189 us
  transfers between devices with their start and end apart: 6, of which 6 were waited for; matrix products, arithmetic and copies ran while one was open for 0% of the time, Pallas kernels for 0%

profile of v1, /device:TPU:1, one launch (start us, length us, event | category | flops | bytes accessed | tf_op | source)
XLA Modules:
  0.0 716.2 jit_solution(7639712770253166810)
XLA Ops:
  7.2 0.0 copy-start
  7.2 0.0 reduce-scatter.2.cloned.1.call-start
  7.2 0.9 copy-done
  8.1 10.3 %fusion.6 = f32[8192,512]{1,0:T(8,128)} fusion(bf16[256,8192]{1,0:T(8,128)(2,1)} %param.6, bf16[256,512]{1,0:T(8,128)(2,1)S(1)} %copy-done), kind=kOutput, calls=%fused_computation.27 | convolution fusion | flops 2147483648 | bytes 21233664 | tf_op jit(solution)/shard_map/dot_general | solution.py:34
  18.4 0.0 copy-start.1
  18.4 0.0 copy-start.2
  18.4 0.0 copy-start.3
  18.4 0.0 reduce-scatter.2.cloned.1.call-update
  18.4 189.3 %reduce-scatter.2.cloned.1.call-done = f32[128,512]{1,0:T(8,128)} async-done(((f32[8192,512]{1,0:T(8,128)}), f32[128,512]{1,0:T(8,128)}) %reduce-scatter.2.cloned.1.call-update) | async-done | bytes 262160 | tf_op jit(solution)/shard_map/reduce_scatter | solution.py:33
  207.7 1.0 slice_select_fusion
  208.7 0.9 collective-permute-start
  209.6 3.0 collective-permute-done
  212.6 1.6 multiply_reduce_fusion.2
  214.2 2.0 pad_maximum_fusion.1
  216.2 129.1 %psum.14 = f32[3]{0:T(128)S(1)} all-reduce(f32[3]{0:T(128)S(1)} %pad_maximum_fusion.1), channel_id=1, replica_groups=mesh['rep'=4,'fsdp'=64] {'fsdp'}, use_global_device_ids=true, to_apply=%region_4.5 | all-reduce | flops 3 | bytes 24 | tf_op jit(solution)/shard_map/psum | solution.py:63
  345.3 1.3 collective-permute-start.1
  346.6 1.2 collective-permute-done.1
  347.8 0.6 fusion.5
  351.0 2.6 collective-permute-start.2
  353.7 2.1 collective-permute-done.2
  355.7 0.6 multiply_reduce_fusion.5
  356.4 2.0 pad_maximum_fusion.2
  358.4 126.3 %psum.15 = f32[3]{0:T(128)S(1)} all-reduce(f32[3]{0:T(128)S(1)} %pad_maximum_fusion.2), channel_id=1, replica_groups=mesh['rep'=4,'fsdp'=64] {'fsdp'}, use_global_device_ids=true, to_apply=%region_8.9 | all-reduce | flops 3 | bytes 24 | tf_op jit(solution)/shard_map/psum | solution.py:63
  484.7 1.3 collective-permute-start.3
  486.0 1.2 collective-permute-done.3
  487.2 2.5 collective-permute-start.4
  489.7 1.3 collective-permute-done.4
  491.1 0.6 fusion.4
  494.3 9.5 %all_gather.3 = f32[128,512]{1,0:T(8,128)S(1)} all-gather(f32[32,512]{1,0:T(8,128)S(1)} %multiply_add_fusion.2), channel_id=1, replica_groups=mesh['rep'=4,'fsdp'=64] {'rep'}, dimensions={0}, use_global_device_ids=true | all-gather | bytes 327680 | tf_op jit(solution)/shard_map/all_gather | solution.py:70
  503.8 0.0 copy-done.1
  503.8 0.0 copy-done.2
  503.9 0.0 copy-done.3
  503.9 1.0 fusion.1
  504.9 1.0 tile.2
  505.9 196.2 %all_to_all.9 = bf16[64,128,512]{2,1,0:T(8,128)(2,1)} all-to-all(bf16[64,128,512]{2,1,0:T(8,128)(2,1)S(1)} %tile.2), channel_id=1, replica_groups=mesh['rep'=4,'fsdp'=64] {'fsdp'}, dimensions={0} | all-to-all | bytes 16777216 | tf_op jit(solution)/shard_map/all_to_all | solution.py:18
  702.1 7.3 %copy.10 = bf16[8192,512]{1,0:T(8,128)(2,1)} copy(bf16[8192,512]{1,0:T(8,128)(2,1)} %bitcast.13) | data formatting | bytes 16777216
  (7 shorter events, 0.1 us)
Async XLA Ops:
  7.2 1.0 copy-start
  7.2 200.5 %reduce-scatter.2.cloned.1.call-start = ((), (), s32[]{:S(2)}) async-start(), calls=%async_computation.2 | async-start | bytes 17039360 | tf_op jit(solution)/shard_map/reduce_scatter | solution.py:33
  18.4 485.4 %copy-start.1 = (f32[128,512]{1,0:T(8,128)S(1)}, f32[128,512]{1,0:T(8,128)}, u32[]{:S(2)}) copy-start(f32[128,512]{1,0:T(8,128)} %param.7) | copy-start | bytes 786436
  18.4 485.4 %copy-start.2 = (f32[128,512]{1,0:T(8,128)S(1)}, f32[128,512]{1,0:T(8,128)}, u32[]{:S(2)}) copy-start(f32[128,512]{1,0:T(8,128)} %param.8) | copy-start | bytes 786436
  18.4 485.5 %copy-start.3 = (f32[128,512]{1,0:T(8,128)S(1)}, f32[128,512]{1,0:T(8,128)}, u32[]{:S(2)}) copy-start(f32[128,512]{1,0:T(8,128)} %param.9) | copy-start | bytes 786436
  208.7 3.9 collective-permute-start
  345.3 2.5 collective-permute-start.1
  351.0 4.7 collective-permute-start.2
  484.7 2.5 collective-permute-start.3
  487.2 3.9 collective-permute-start.4
Sparse Core Ops, SparseCore 0:
  18.6 189.1 reduce-scatter.1
